TPU v7x, 32 devices: a whole 2x2x4 slice. The times are simulated.
32 devices in a mesh: sim: 2 (over y), grp: 4 (over z), gz: 4 (over x, core).
Axes of the slice: x: 2, y: 2, z: 4, core: 2. Of those that a mesh axis runs over, the one named last changes fastest.
Arguments:
- fields: float32 [8, 2, 1024, 1024], P(None, None, 'sim', ('grp', 'gz')), may hold values from -6 to 6
- diffusivity: float32 [8], replicated, may hold values from 0.03 to 0.12
- velocity: float32 [2, 8], replicated, may hold values from -0.4 to 0.4
- coupling: float32 [8, 8], replicated, may hold values from -0.6 to 0.6
- basis_x: bfloat16 [1024, 128], replicated, may hold values from -0.1875 to 0.1875
- basis_y: bfloat16 [1024, 128], replicated, may hold values from -0.1875 to 0.1875
Outputs:
- fields_out: float32 [8, 2, 1024, 1024], P(None, None, 'sim', ('grp', 'gz'))
- gram_x: float32 [1024, 1024], P('sim', ('grp', 'gz'))
- gram_y: float32 [1024, 1024], P(('grp', 'gz'), 'sim')
- core: float32 [8, 2, 128, 128], P(None, None, 'sim', ('grp', 'gz'))
All inputs are finite; a program needn't handle non-finite values.
Results may differ from a plain program's by a relative error of at most 0.0003.
Values sent between devices are 32-bit elements; how exact they have to be, the bound alone decides.
No kernel may reach another device: no remote copies, remote signals or barrier semaphores. Data moves between devices by JAX's collectives and lax.ppermute only.
A program may use at most 64 MiB of HBM per device.

v0:
```python
import jax
import jax.numpy as jnp
from jax import lax
from jax.sharding import PartitionSpec as P

NY = 1024
RANK = 128
STEPS = 2
time_step = 1.0
highest = lax.Precision.HIGHEST


def with_halo(cells, sides, width):
    for axis, dim in sides:
        count = lax.axis_size(axis)
        head = lax.slice_in_dim(cells, 0, width, axis=dim)
        tail = lax.slice_in_dim(cells, cells.shape[dim] - width, cells.shape[dim], axis=dim)
        cells = jnp.concatenate(
            [
                lax.ppermute(tail, axis, [(i, (i + 1) % count) for i in range(count)]),
                cells,
                lax.ppermute(head, axis, [((i + 1) % count, i) for i in range(count)]),
            ],
            axis=dim,
        )
    return cells


def rates(state, diffusivity, velocity, coupling):
    padded = with_halo(state, (("sim", 2), (("grp", "gz"), 3)), 1)
    center = padded[:, :, 1:-1, 1:-1]
    x_plus = padded[:, :, 2:, 1:-1]
    x_minus = padded[:, :, :-2, 1:-1]
    y_plus = padded[:, :, 1:-1, 2:]
    y_minus = padded[:, :, 1:-1, :-2]
    z_plus = jnp.roll(center, -1, 1)
    z_minus = jnp.roll(center, 1, 1)
    lapl = -6.0 * center + z_plus + z_minus + x_plus + x_minus + y_plus + y_minus
    grad_x = (x_plus - x_minus) * 0.5
    grad_y = (y_plus - y_minus) * 0.5
    react = jnp.einsum("fg,gzxy->fzxy", coupling, jnp.tanh(center), precision=highest)
    return (
        diffusivity[:, None, None, None] * lapl
        - velocity[0][:, None, None, None] * grad_x
        - velocity[1][:, None, None, None] * grad_y
        + react
    )


def shards(fields, diffusivity, velocity, coupling, basis_x, basis_y):
    state = fields
    for repeat in range(STEPS):
        first = rates(state, diffusivity, velocity, coupling)
        second = rates(state + 0.5 * time_step * first, diffusivity, velocity, coupling)
        third = rates(state + 0.5 * time_step * second, diffusivity, velocity, coupling)
        fourth = rates(state + time_step * third, diffusivity, velocity, coupling)
        state = state + time_step / 6.0 * (first + 2.0 * second + 2.0 * third + fourth)
    nfield = state.shape[0]
    depth = state.shape[1]
    x_rows = state.shape[2]
    basis_xf = basis_x.astype(jnp.float32)
    basis_yf = basis_y.astype(jnp.float32)
    block = jnp.einsum(
        "fzxy,fzwy->xw", state, lax.all_gather(state, "sim", axis=2, tiled=True), precision=highest
    )
    gram_rows = block
    own_basis = lax.dynamic_slice_in_dim(basis_xf, lax.axis_index("sim") * x_rows, x_rows, 0)
    partial_proj = jnp.einsum("xr,fzxy->fzry", own_basis, state, precision=highest)
    projected = lax.psum_scatter(partial_proj, "sim", scatter_dimension=2, tiled=True)
    gram_x = lax.psum_scatter(gram_rows, ("grp", "gz"), scatter_dimension=1, tiled=True) / (
        nfield * depth * NY
    )
    rank_grp = RANK // lax.axis_size(("grp", "gz"))
    rank_cols_y = lax.dynamic_slice_in_dim(
        basis_yf, lax.axis_index(("grp", "gz")) * rank_grp, rank_grp, 1
    )
    incoming = lax.all_gather(projected, ("grp", "gz"), axis=3, tiled=True)
    block = jnp.einsum("fzry,fzrv->yv", projected, incoming, precision=highest)
    core_part = jnp.einsum("vs,fzrv->fzrs", rank_cols_y, incoming, precision=highest)
    gram_y = lax.psum_scatter(block, "sim", scatter_dimension=1, tiled=True) / (
        nfield * depth * RANK
    )
    return (state, gram_x, gram_y, core_part)


def solution(mesh):
    in_specs = (P(None, None, "sim", ("grp", "gz")), P(), P(), P(), P(), P())
    out_specs = (
        P(None, None, "sim", ("grp", "gz")),
        P("sim", ("grp", "gz")),
        P(("grp", "gz"), "sim"),
        P(None, None, "sim", ("grp", "gz")),
    )
    return jax.shard_map(shards, mesh=mesh, in_specs=in_specs, out_specs=out_specs, check_vma=False)
```

profile of v0, /device:TPU:0, one launch (start us, length us, event | category | flops | bytes accessed | tf_op | source)
XLA Modules:
  0.0 532.1 jit_solution(15932883289345783442)
XLA Ops:
  7.2 2.8 copy.61
  10.3 3.1 collective-permute-start
  13.6 12.5 %collective-permute-done = f32[8,2,1,64]{2,0,3,1:T(8,128)S(1)} collective-permute-done((f32[8,2,1,64]{2,0,3,1:T(8,128)S(1)}, f32[8,2,1,64]{2,0,3,1:T(8,128)S(1)}, u32[]{:S(2)}, u32[]{:S(2)}) %collective-permute-start) | collective-permute-done | bytes 4128 | tf_op jit(solution)/shard_map/ppermute | solution.py:22
  26.1 10.4 %collective-permute-done.1 = f32[8,2,1,64]{2,0,3,1:T(8,128)S(1)} collective-permute-done((f32[8,2,1,64]{2,0,3,1:T(8,128)S(1)}, f32[8,2,1,64]{2,0,3,1:T(8,128)S(1)}, u32[]{:S(2)}, u32[]{:S(2)}) %collective-permute-start.1) | collective-permute-done | bytes 4128 | tf_op jit(solution)/shard_map/ppermute | solution.py:20
  36.6 3.4 collective-permute-start.2
  41.6 4.4 collective-permute-done.3
  46.1 5.2 multiply_add_fusion.3
  51.5 1.6 collective-permute-start.4
  53.6 12.5 %collective-permute-done.4 = f32[8,2,1,64]{2,0,3,1:T(8,128)S(1)} collective-permute-done((f32[8,2,1,64]{2,0,3,1:T(8,128)S(1)}, f32[8,2,1,64]{2,0,3,1:T(8,128)S(1)}, u32[]{:S(2)}, u32[]{:S(2)}) %collective-permute-start.4) | collective-permute-done | bytes 4128 | tf_op jit(solution)/shard_map/ppermute | solution.py:22
  66.1 5.6 %collective-permute-done.5 = f32[8,2,1,64]{2,0,3,1:T(8,128)S(1)} collective-permute-done((f32[8,2,1,64]{2,0,3,1:T(8,128)S(1)}, f32[8,2,1,64]{2,0,3,1:T(8,128)S(1)}, u32[]{:S(2)}, u32[]{:S(2)}) %collective-permute-start.5) | collective-permute-done | bytes 4128 | tf_op jit(solution)/shard_map/ppermute | solution.py:20
  71.9 4.1 collective-permute-start.6
  77.7 4.6 collective-permute-done.7
  82.3 4.5 multiply_add_fusion.2
  87.0 1.6 collective-permute-start.8
  89.1 12.5 %collective-permute-done.8 = f32[8,2,1,64]{2,0,3,1:T(8,128)S(1)} collective-permute-done((f32[8,2,1,64]{2,0,3,1:T(8,128)S(1)}, f32[8,2,1,64]{2,0,3,1:T(8,128)S(1)}, u32[]{:S(2)}, u32[]{:S(2)}) %collective-permute-start.8) | collective-permute-done | bytes 4128 | tf_op jit(solution)/shard_map/ppermute | solution.py:22
  101.6 5.6 %collective-permute-done.9 = f32[8,2,1,64]{2,0,3,1:T(8,128)S(1)} collective-permute-done((f32[8,2,1,64]{2,0,3,1:T(8,128)S(1)}, f32[8,2,1,64]{2,0,3,1:T(8,128)S(1)}, u32[]{:S(2)}, u32[]{:S(2)}) %collective-permute-start.9) | collective-permute-done | bytes 4128 | tf_op jit(solution)/shard_map/ppermute | solution.py:20
  107.3 2.7 collective-permute-start.10
  110.2 1.5 collective-permute-done.10
  111.7 4.4 collective-permute-done.11
  116.1 4.9 copy_add_fusion
  121.2 1.6 collective-permute-start.12
  123.3 12.5 %collective-permute-done.12 = f32[8,2,1,64]{2,0,3,1:T(8,128)S(1)} collective-permute-done((f32[8,2,1,64]{2,0,3,1:T(8,128)S(1)}, f32[8,2,1,64]{2,0,3,1:T(8,128)S(1)}, u32[]{:S(2)}, u32[]{:S(2)}) %collective-permute-start.12) | collective-permute-done | bytes 4128 | tf_op jit(solution)/shard_map/ppermute | solution.py:22
  135.8 5.6 %collective-permute-done.13 = f32[8,2,1,64]{2,0,3,1:T(8,128)S(1)} collective-permute-done((f32[8,2,1,64]{2,0,3,1:T(8,128)S(1)}, f32[8,2,1,64]{2,0,3,1:T(8,128)S(1)}, u32[]{:S(2)}, u32[]{:S(2)}) %collective-permute-start.13) | collective-permute-done | bytes 4128 | tf_op jit(solution)/shard_map/ppermute | solution.py:20
  144.5 4.6 collective-permute-done.15
  149.2 5.1 fusion.36
  154.5 1.6 collective-permute-start.16
  156.6 12.5 %collective-permute-done.16 = f32[8,2,1,64]{2,0,3,1:T(8,128)S(1)} collective-permute-done((f32[8,2,1,64]{2,0,3,1:T(8,128)S(1)}, f32[8,2,1,64]{2,0,3,1:T(8,128)S(1)}, u32[]{:S(2)}, u32[]{:S(2)}) %collective-permute-start.16) | collective-permute-done | bytes 4128 | tf_op jit(solution)/shard_map/ppermute | solution.py:22
  169.1 5.6 %collective-permute-done.17 = f32[8,2,1,64]{2,0,3,1:T(8,128)S(1)} collective-permute-done((f32[8,2,1,64]{2,0,3,1:T(8,128)S(1)}, f32[8,2,1,64]{2,0,3,1:T(8,128)S(1)}, u32[]{:S(2)}, u32[]{:S(2)}) %collective-permute-start.17) | collective-permute-done | bytes 4128 | tf_op jit(solution)/shard_map/ppermute | solution.py:20
  176.0 1.5 collective-permute-done.18
  177.5 4.4 collective-permute-done.19
  181.9 5.4 %multiply_add_fusion.1 = (f32[8,2,512,64]{2,0,3,1:T(8,128)S(1)}, f32[8,2,512,64]{2,0,3,1:T(8,128)}) fusion(f32[8,2,512,64]{2,0,3,1:T(8,128)S(1)} %fusion.36, f32[8,8]{1,0:T(8,128)S(1)} %copy-done.9, f32[8]{0:T(128)S(1)} %get-tuple-element.65, f32[8]{0:T(128)S(1)} %get-tuple-element.64, f32[8,2,1,64]{2,0,3,1:T(8,128)S(1)} %collective-permute-done.16, ...), kind=kOutput, calls=%fused_computation.154 | convolution fusion | flops 63963136 | bytes 8462944 | tf_op jit(solution)/shard_map/fg,gzxy->fzxy/dot_general | solution.py:41
  187.5 1.6 collective-permute-start.20
  189.6 12.5 %collective-permute-done.20 = f32[8,2,1,64]{2,0,3,1:T(8,128)S(1)} collective-permute-done((f32[8,2,1,64]{2,0,3,1:T(8,128)S(1)}, f32[8,2,1,64]{2,0,3,1:T(8,128)S(1)}, u32[]{:S(2)}, u32[]{:S(2)}) %collective-permute-start.20) | collective-permute-done | bytes 4128 | tf_op jit(solution)/shard_map/ppermute | solution.py:22
  202.1 5.6 %collective-permute-done.21 = f32[8,2,1,64]{2,0,3,1:T(8,128)S(1)} collective-permute-done((f32[8,2,1,64]{2,0,3,1:T(8,128)S(1)}, f32[8,2,1,64]{2,0,3,1:T(8,128)S(1)}, u32[]{:S(2)}, u32[]{:S(2)}) %collective-permute-start.21) | collective-permute-done | bytes 4128 | tf_op jit(solution)/shard_map/ppermute | solution.py:20
  209.2 1.5 collective-permute-done.22
  210.7 4.4 collective-permute-done.23
  215.1 5.5 %multiply_add_fusion = (f32[8,2,512,64]{2,0,3,1:T(8,128)S(1)}, f32[8,2,512,64]{2,0,3,1:T(8,128)}) fusion(f32[8,2,512,64]{2,0,3,1:T(8,128)S(1)} %fusion.36, f32[8,8]{1,0:T(8,128)S(1)} %copy-done.9, f32[8,2,512,64]{2,0,3,1:T(8,128)S(1)} %get-tuple-element.72, f32[8]{0:T(128)S(1)} %get-tuple-element.65, f32[8]{0:T(128)S(1)} %get-tuple-element.64, ...), kind=kOutput, calls=%fused_computation.151 | convolution fusion | flops 63963136 | bytes 10560096 | tf_op jit(solution)/shard_map/fg,gzxy->fzxy/dot_general | solution.py:41
  220.9 1.6 collective-permute-start.24
  223.0 12.5 %collective-permute-done.24 = f32[8,2,1,64]{2,0,3,1:T(8,128)S(1)} collective-permute-done((f32[8,2,1,64]{2,0,3,1:T(8,128)S(1)}, f32[8,2,1,64]{2,0,3,1:T(8,128)S(1)}, u32[]{:S(2)}, u32[]{:S(2)}) %collective-permute-start.24) | collective-permute-done | bytes 4128 | tf_op jit(solution)/shard_map/ppermute | solution.py:22
  235.5 5.6 %collective-permute-done.25 = f32[8,2,1,64]{2,0,3,1:T(8,128)S(1)} collective-permute-done((f32[8,2,1,64]{2,0,3,1:T(8,128)S(1)}, f32[8,2,1,64]{2,0,3,1:T(8,128)S(1)}, u32[]{:S(2)}, u32[]{:S(2)}) %collective-permute-start.25) | collective-permute-done | bytes 4128 | tf_op jit(solution)/shard_map/ppermute | solution.py:20
  241.2 1.9 collective-permute-start.26
  244.8 4.8 collective-permute-done.27
  249.7 5.6 %fusion.158 = (f32[8,2,512,64]{2,0,3,1:T(8,128)S(1)}, f32[8,2,512,64]{2,0,3,1:T(8,128)}) fusion(f32[8,2,512,64]{2,0,3,1:T(8,128)S(1)} %fusion.36, f32[8,8]{1,0:T(8,128)S(1)} %copy-done.9, f32[8,2,512,64]{2,0,3,1:T(8,128)S(1)} %get-tuple-element.74, f32[8]{0:T(128)S(1)} %get-tuple-element.65, f32[8]{0:T(128)S(1)} %get-tuple-element.64, ...), kind=kOutput, calls=%fused_computation.229 | convolution fusion | flops 63438848 | bytes 10560096 | tf_op jit(solution)/shard_map/fg,gzxy->fzxy/dot_general | solution.py:41
  256.6 1.5 collective-permute-start.28
  258.7 12.7 %collective-permute-done.28 = f32[8,2,1,64]{2,0,3,1:T(8,128)S(1)} collective-permute-done((f32[8,2,1,64]{2,0,3,1:T(8,128)}, f32[8,2,1,64]{2,0,3,1:T(8,128)S(1)}, u32[]{:S(2)}, u32[]{:S(2)}) %collective-permute-start.28) | collective-permute-done | bytes 4128 | tf_op jit(solution)/shard_map/ppermute | solution.py:22
  271.4 5.6 %collective-permute-done.29 = f32[8,2,1,64]{2,0,3,1:T(8,128)S(1)} collective-permute-done((f32[8,2,1,64]{2,0,3,1:T(8,128)}, f32[8,2,1,64]{2,0,3,1:T(8,128)S(1)}, u32[]{:S(2)}, u32[]{:S(2)}) %collective-permute-start.29) | collective-permute-done | bytes 4128 | tf_op jit(solution)/shard_map/ppermute | solution.py:20
  277.1 1.8 collective-permute-start.30
  280.5 4.5 collective-permute-done.31
  285.0 8.8 %fusion.71 = f32[8,2,512,64]{2,0,3,1:T(8,128)S(1)} fusion(f32[8,2,512,64]{2,0,3,1:T(8,128)S(1)} %copy-done.4, f32[8,1,512,64]{2,0,3,1:T(8,128)S(1)} %get-tuple-element.35, f32[8,1,512,64]{2,0,3,1:T(8,128)S(1)} %get-tuple-element.34, f32[8,2,514,1]{2,0,3,1:T(8,128)S(1)} %collective-permute-done.30, f32[8,2,1,64]{2,0,3,1:T(8,128)S(1)} %collective-permute-done.28, ...), kind=kOutput, calls=%fused_computation.79 | convolution fusion | flops 66584576 | bytes 14754400 | tf_op jit(solution)/shard_map/fg,gzxy->fzxy/dot_general | solution.py:41
  293.9 1.9 convolution_bitcast_fusion
  295.8 1.9 copy.75
  297.7 1.8 reshape.20
  300.3 11.4 %reduce-scatter.10.cloned.1.call-done = f32[64,1024]{1,0:T(8,128)} async-done(((f32[128,1024]{1,0:T(8,128)}), f32[64,1024]{1,0:T(8,128)}) %reduce-scatter.10.cloned.1.call-update) | async-done | bytes 262160
  314.5 56.1 %all-gather.3.cloned.1.call-done = f32[8,2,1024,64]{2,0,3,1:T(8,128)} async-done(((f32[8,2,512,64]{2,0,3,1:T(8,128)}), f32[8,2,1024,64]{2,0,3,1:T(8,128)}) %all-gather.3.cloned.1.call-update) | async-done | bytes 4194320 | tf_op jit(solution)/shard_map/all_gather | solution.py:64
  370.5 9.7 %fusion.89 = f32[512,1024]{0,1:T(8,128)} fusion(f32[8,2,1024,64]{2,0,3,1:T(8,128)} %all-gather.3.cloned.1.call-done, f32[8,2,512,64]{2,0,3,1:T(8,128)S(1)} %copy-done.2), kind=kOutput, calls=%fused_computation.165 | convolution fusion | flops 6442450944 | bytes 8388608 | tf_op jit(solution)/shard_map/fzxy,fzwy->xw/dot_general | solution.py:63
  380.3 2.5 copy.69
  382.8 64.2 %all-gather.5.cloned.1.call-done = f32[8,2,64,1024]{2,0,1,3:T(8,128)} async-done(((f32[8,2,64,64]{2,0,1,3:T(8,128)}), f32[8,2,64,1024]{2,0,1,3:T(8,128)}) %all-gather.5.cloned.1.call-update) | async-done | bytes 4194320 | tf_op jit(solution)/shard_map/all_gather | solution.py:77
  447.0 6.9 %copy.66 = f32[8,2,64,1024]{3,2,1,0:T(8,128)} copy(f32[8,2,64,1024]{2,0,1,3:T(8,128)} %all-gather.5.cloned.1.call-done) | data formatting | bytes 8388608 | tf_op jit(solution)/shard_map/all_gather | solution.py:77
  453.9 5.8 %convolution_bitcast_fusion.1 = f32[64,1024]{1,0:T(8,128)} fusion(f32[8,2,64,1024]{3,2,1,0:T(8,128)} %copy.66, f32[8,2,64,64]{3,1,0,2:T(2,128)S(1)} %bitcast.93), kind=kOutput, calls=%fused_computation.167 | convolution fusion | flops 805306368 | bytes 4718592 | tf_op jit(solution)/shard_map/fzry,fzrv->yv/dot_general | solution.py:78
  459.7 51.4 %reduce-scatter.6.cloned.1.call-done = f32[512,64]{0,1:T(8,128)} async-done(((f32[512,1024]{0,1:T(8,128)}), f32[512,64]{0,1:T(8,128)}) %reduce-scatter.6.cloned.1.call-update) | async-done | bytes 131088 | tf_op jit(solution)/shard_map/reduce_scatter | solution.py:70
  511.0 1.6 broadcast_multiply_fusion.1
  512.6 5.5 %fusion.95 = f32[8,2,64,8]{2,3,1,0:T(8,128)} fusion(f32[8,2,64,1024]{3,2,1,0:T(8,128)} %copy.66, bf16[1024,128]{1,0:T(8,128)(2,1)S(1)} %copy-done.7, s32[]{:T(128)S(6)} %select_n.7), kind=kOutput, calls=%fused_computation.169 | convolution fusion | flops 100663296 | bytes 4489220 | tf_op jit(solution)/shard_map/vs,fzrv->fzrs/dot_general | solution.py:79
  518.0 5.8 %reduce-scatter.8.cloned.1.call-done = f32[64,512]{1,0:T(8,128)} async-done(((f32[64,1024]{1,0:T(8,128)}), f32[64,512]{1,0:T(8,128)}) %reduce-scatter.8.cloned.1.call-update) | async-done | bytes 131088 | tf_op jit(solution)/shard_map/reduce_scatter | solution.py:80
  523.8 1.6 broadcast_multiply_fusion
  (88 shorter events, 23.2 us)
Async XLA Ops:
  7.2 286.7 %copy-start = (bf16[1024,128]{1,0:T(8,128)(2,1)S(1)}, bf16[1024,128]{1,0:T(8,128)(2,1)}, u32[]{:S(2)}) copy-start(bf16[1024,128]{1,0:T(8,128)(2,1)} %param.10) | copy-start | bytes 786436
  7.2 304.5 %reduce-scatter.10.cloned.1.call-start = ((), (), s32[]{:S(2)}) async-start(), calls=%async_computation.7 | async-start | bytes 786432
  10.3 15.8 %collective-permute-start = (f32[8,2,1,64]{2,0,3,1:T(8,128)S(1)}, f32[8,2,1,64]{2,0,3,1:T(8,128)S(1)}, u32[]{:S(2)}, u32[]{:S(2)}) collective-permute-start(f32[8,2,1,64]{2,0,3,1:T(8,128)S(1)} %get-tuple-element.61), channel_id=1, source_target_pairs={{16,0},{0,16},{17,1},{1,17},{18,2},{2,18},{19,3},{3,19},{20,4},{4,... | collective-permute-start | bytes 12296 | tf_op jit(solution)/shard_map/ppermute | solution.py:22
  13.3 23.2 %collective-permute-start.1 = (f32[8,2,1,64]{2,0,3,1:T(8,128)S(1)}, f32[8,2,1,64]{2,0,3,1:T(8,128)S(1)}, u32[]{:S(2)}, u32[]{:S(2)}) collective-permute-start(f32[8,2,1,64]{2,0,3,1:T(8,128)S(1)} %get-tuple-element.60), channel_id=1, source_target_pairs={{0,16},{16,0},{1,17},{17,1},{2,18},{18,2},{3,19},{19,3},{4,20},{20... | collective-permute-start | bytes 12296 | tf_op jit(solution)/shard_map/ppermute | solution.py:20
  13.6 26.4 %copy-start.8 = (f32[2,8]{1,0:T(2,128)S(1)}, f32[2,8]{1,0:T(2,128)}, u32[]{:S(2)}) copy-start(f32[2,8]{1,0:T(2,128)} %param.8) | copy-start | bytes 196
  13.6 26.4 %copy-start.6 = (f32[8,2,512,64]{2,3,1,0:T(8,128)S(1)}, f32[8,2,512,64]{2,3,1,0:T(8,128)}, u32[]{:S(2)}) copy-start(f32[8,2,512,64]{2,3,1,0:T(8,128)} %param.6) | copy-start | bytes 6291460
  36.6 5.1 collective-permute-start.2
  40.0 6.1 %collective-permute-start.3 = (f32[8,2,514,1]{2,0,3,1:T(8,128)S(1)}, f32[8,2,514,1]{2,0,3,1:T(8,128)S(1)}, u32[]{:S(2)}, u32[]{:S(2)}) collective-permute-start(f32[8,2,514,1]{2,0,3,1:T(8,128)S(1)} %get-tuple-element.30), channel_id=1, source_target_pairs={{0,1},{1,2},{2,3},{3,4},{4,5},{5,6},{6,7},{7,8},{8,9},{9,10},{10,1... | collective-permute-start | bytes 98696 | tf_op jit(solution)/shard_map/ppermute | solution.py:20
  40.0 6.1 %copy-start.9 = (f32[8,8]{1,0:T(8,128)S(1)}, f32[8,8]{1,0:T(8,128)}, u32[]{:S(2)}) copy-start(f32[8,8]{1,0:T(8,128)} %param.9) | copy-start | bytes 772
  40.0 6.1 %copy-start.10 = (f32[8]{0:T(128)S(1)}, f32[8]{0:T(128)}, u32[]{:S(2)}) copy-start(f32[8]{0:T(128)} %param.7) | copy-start | bytes 100
  51.5 14.6 %collective-permute-start.4 = (f32[8,2,1,64]{2,0,3,1:T(8,128)S(1)}, f32[8,2,1,64]{2,0,3,1:T(8,128)S(1)}, u32[]{:S(2)}, u32[]{:S(2)}) collective-permute-start(f32[8,2,1,64]{2,0,3,1:T(8,128)S(1)} %get-tuple-element.57), channel_id=1, source_target_pairs={{16,0},{0,16},{17,1},{1,17},{18,2},{2,18},{19,3},{3,19},{20,4},{4,... | collective-permute-start | bytes 12296 | tf_op jit(solution)/shard_map/ppermute | solution.py:22
  53.1 18.6 %collective-permute-start.5 = (f32[8,2,1,64]{2,0,3,1:T(8,128)S(1)}, f32[8,2,1,64]{2,0,3,1:T(8,128)S(1)}, u32[]{:S(2)}, u32[]{:S(2)}) collective-permute-start(f32[8,2,1,64]{2,0,3,1:T(8,128)S(1)} %get-tuple-element.56), channel_id=1, source_target_pairs={{0,16},{16,0},{1,17},{17,1},{2,18},{18,2},{3,19},{19,3},{4,20},{20... | collective-permute-start | bytes 12296 | tf_op jit(solution)/shard_map/ppermute | solution.py:20
  71.9 5.8 %collective-permute-start.6 = (f32[8,2,514,1]{2,0,3,1:T(8,128)S(1)}, f32[8,2,514,1]{2,0,3,1:T(8,128)S(1)}, u32[]{:S(2)}, u32[]{:S(2)}) collective-permute-start(f32[8,2,514,1]{2,0,3,1:T(8,128)S(1)} %get-tuple-element.29), channel_id=1, source_target_pairs={{1,0},{2,1},{3,2},{4,3},{5,4},{6,5},{7,6},{8,7},{9,8},{10,9},{11,1... | collective-permute-start | bytes 98696 | tf_op jit(solution)/shard_map/ppermute | solution.py:22
  76.0 6.3 %collective-permute-start.7 = (f32[8,2,514,1]{2,0,3,1:T(8,128)S(1)}, f32[8,2,514,1]{2,0,3,1:T(8,128)S(1)}, u32[]{:S(2)}, u32[]{:S(2)}) collective-permute-start(f32[8,2,514,1]{2,0,3,1:T(8,128)S(1)} %get-tuple-element.28), channel_id=1, source_target_pairs={{0,1},{1,2},{2,3},{3,4},{4,5},{5,6},{6,7},{7,8},{8,9},{9,10},{10,1... | collective-permute-start | bytes 98696 | tf_op jit(solution)/shard_map/ppermute | solution.py:20
  87.0 14.6 %collective-permute-start.8 = (f32[8,2,1,64]{2,0,3,1:T(8,128)S(1)}, f32[8,2,1,64]{2,0,3,1:T(8,128)S(1)}, u32[]{:S(2)}, u32[]{:S(2)}) collective-permute-start(f32[8,2,1,64]{2,0,3,1:T(8,128)S(1)} %get-tuple-element.53), channel_id=1, source_target_pairs={{16,0},{0,16},{17,1},{1,17},{18,2},{2,18},{19,3},{3,19},{20,4},{4,... | collective-permute-start | bytes 12296 | tf_op jit(solution)/shard_map/ppermute | solution.py:22
  88.6 18.6 %collective-permute-start.9 = (f32[8,2,1,64]{2,0,3,1:T(8,128)S(1)}, f32[8,2,1,64]{2,0,3,1:T(8,128)S(1)}, u32[]{:S(2)}, u32[]{:S(2)}) collective-permute-start(f32[8,2,1,64]{2,0,3,1:T(8,128)S(1)} %get-tuple-element.52), channel_id=1, source_target_pairs={{0,16},{16,0},{1,17},{17,1},{2,18},{18,2},{3,19},{19,3},{4,20},{20... | collective-permute-start | bytes 12296 | tf_op jit(solution)/shard_map/ppermute | solution.py:20
  107.3 4.3 collective-permute-start.10
  110.0 6.1 %collective-permute-start.11 = (f32[8,2,514,1]{2,0,3,1:T(8,128)S(1)}, f32[8,2,514,1]{2,0,3,1:T(8,128)S(1)}, u32[]{:S(2)}, u32[]{:S(2)}) collective-permute-start(f32[8,2,514,1]{2,0,3,1:T(8,128)S(1)} %get-tuple-element.26), channel_id=1, source_target_pairs={{0,1},{1,2},{2,3},{3,4},{4,5},{5,6},{6,7},{7,8},{8,9},{9,10},{10,1... | collective-permute-start | bytes 98696 | tf_op jit(solution)/shard_map/ppermute | solution.py:20
  121.2 14.6 %collective-permute-start.12 = (f32[8,2,1,64]{2,0,3,1:T(8,128)S(1)}, f32[8,2,1,64]{2,0,3,1:T(8,128)S(1)}, u32[]{:S(2)}, u32[]{:S(2)}) collective-permute-start(f32[8,2,1,64]{2,0,3,1:T(8,128)S(1)} %get-tuple-element.49), channel_id=1, source_target_pairs={{16,0},{0,16},{17,1},{1,17},{18,2},{2,18},{19,3},{3,19},{20,4},{4,... | collective-permute-start | bytes 12296 | tf_op jit(solution)/shard_map/ppermute | solution.py:22
  122.8 18.6 %collective-permute-start.13 = (f32[8,2,1,64]{2,0,3,1:T(8,128)S(1)}, f32[8,2,1,64]{2,0,3,1:T(8,128)S(1)}, u32[]{:S(2)}, u32[]{:S(2)}) collective-permute-start(f32[8,2,1,64]{2,0,3,1:T(8,128)S(1)} %get-tuple-element.48), channel_id=1, source_target_pairs={{0,16},{16,0},{1,17},{17,1},{2,18},{18,2},{3,19},{19,3},{4,20},{20... | collective-permute-start | bytes 12296 | tf_op jit(solution)/shard_map/ppermute | solution.py:20
  141.5 3.0 collective-permute-start.14
  142.9 6.3 %collective-permute-start.15 = (f32[8,2,514,1]{2,0,3,1:T(8,128)S(1)}, f32[8,2,514,1]{2,0,3,1:T(8,128)S(1)}, u32[]{:S(2)}, u32[]{:S(2)}) collective-permute-start(f32[8,2,514,1]{2,0,3,1:T(8,128)S(1)} %get-tuple-element.24), channel_id=1, source_target_pairs={{0,1},{1,2},{2,3},{3,4},{4,5},{5,6},{6,7},{7,8},{8,9},{9,10},{10,1... | collective-permute-start | bytes 98696 | tf_op jit(solution)/shard_map/ppermute | solution.py:20
  154.3 95.4 %copy-start.3 = (f32[8,2,512,64]{2,0,3,1:T(8,128)}, f32[8,2,512,64]{2,0,3,1:T(8,128)S(1)}, u32[]{:S(2)}) copy-start(f32[8,2,512,64]{2,0,3,1:T(8,128)S(1)} %fusion.36) | copy-start | bytes 6291460
  154.5 14.6 %collective-permute-start.16 = (f32[8,2,1,64]{2,0,3,1:T(8,128)S(1)}, f32[8,2,1,64]{2,0,3,1:T(8,128)S(1)}, u32[]{:S(2)}, u32[]{:S(2)}) collective-permute-start(f32[8,2,1,64]{2,0,3,1:T(8,128)S(1)} %get-tuple-element.45), channel_id=1, source_target_pairs={{16,0},{0,16},{17,1},{1,17},{18,2},{2,18},{19,3},{3,19},{20,4},{4,... | collective-permute-start | bytes 12296 | tf_op jit(solution)/shard_map/ppermute | solution.py:22
  156.1 18.6 %collective-permute-start.17 = (f32[8,2,1,64]{2,0,3,1:T(8,128)S(1)}, f32[8,2,1,64]{2,0,3,1:T(8,128)S(1)}, u32[]{:S(2)}, u32[]{:S(2)}) collective-permute-start(f32[8,2,1,64]{2,0,3,1:T(8,128)S(1)} %get-tuple-element.44), channel_id=1, source_target_pairs={{0,16},{16,0},{1,17},{17,1},{2,18},{18,2},{3,19},{19,3},{4,20},{20... | collective-permute-start | bytes 12296 | tf_op jit(solution)/shard_map/ppermute | solution.py:20
  174.8 2.6 collective-permute-start.18
  175.8 6.1 %collective-permute-start.19 = (f32[8,2,514,1]{2,0,3,1:T(8,128)S(1)}, f32[8,2,514,1]{2,0,3,1:T(8,128)S(1)}, u32[]{:S(2)}, u32[]{:S(2)}) collective-permute-start(f32[8,2,514,1]{2,0,3,1:T(8,128)S(1)} %get-tuple-element.22), channel_id=1, source_target_pairs={{0,1},{1,2},{2,3},{3,4},{4,5},{5,6},{6,7},{7,8},{8,9},{9,10},{10,1... | collective-permute-start | bytes 98696 | tf_op jit(solution)/shard_map/ppermute | solution.py:20
  187.5 14.6 %collective-permute-start.20 = (f32[8,2,1,64]{2,0,3,1:T(8,128)S(1)}, f32[8,2,1,64]{2,0,3,1:T(8,128)S(1)}, u32[]{:S(2)}, u32[]{:S(2)}) collective-permute-start(f32[8,2,1,64]{2,0,3,1:T(8,128)S(1)} %get-tuple-element.41), channel_id=1, source_target_pairs={{16,0},{0,16},{17,1},{1,17},{18,2},{2,18},{19,3},{3,19},{20,4},{4,... | collective-permute-start | bytes 12296 | tf_op jit(solution)/shard_map/ppermute | solution.py:22
  189.1 18.6 %collective-permute-start.21 = (f32[8,2,1,64]{2,0,3,1:T(8,128)S(1)}, f32[8,2,1,64]{2,0,3,1:T(8,128)S(1)}, u32[]{:S(2)}, u32[]{:S(2)}) collective-permute-start(f32[8,2,1,64]{2,0,3,1:T(8,128)S(1)} %get-tuple-element.40), channel_id=1, source_target_pairs={{0,16},{16,0},{1,17},{17,1},{2,18},{18,2},{3,19},{19,3},{4,20},{20... | collective-permute-start | bytes 12296 | tf_op jit(solution)/shard_map/ppermute | solution.py:20
  207.9 2.8 collective-permute-start.22
  209.0 6.1 %collective-permute-start.23 = (f32[8,2,514,1]{2,0,3,1:T(8,128)S(1)}, f32[8,2,514,1]{2,0,3,1:T(8,128)S(1)}, u32[]{:S(2)}, u32[]{:S(2)}) collective-permute-start(f32[8,2,514,1]{2,0,3,1:T(8,128)S(1)} %get-tuple-element.20), channel_id=1, source_target_pairs={{0,1},{1,2},{2,3},{3,4},{4,5},{5,6},{6,7},{7,8},{8,9},{9,10},{10,1... | collective-permute-start | bytes 98696 | tf_op jit(solution)/shard_map/ppermute | solution.py:20
  220.9 14.6 %collective-permute-start.24 = (f32[8,2,1,64]{2,0,3,1:T(8,128)S(1)}, f32[8,2,1,64]{2,0,3,1:T(8,128)S(1)}, u32[]{:S(2)}, u32[]{:S(2)}) collective-permute-start(f32[8,2,1,64]{2,0,3,1:T(8,128)S(1)} %get-tuple-element.37), channel_id=1, source_target_pairs={{16,0},{0,16},{17,1},{1,17},{18,2},{2,18},{19,3},{3,19},{20,4},{4,... | collective-permute-start | bytes 12296 | tf_op jit(solution)/shard_map/ppermute | solution.py:22
  222.5 18.6 %collective-permute-start.25 = (f32[8,2,1,64]{2,0,3,1:T(8,128)S(1)}, f32[8,2,1,64]{2,0,3,1:T(8,128)S(1)}, u32[]{:S(2)}, u32[]{:S(2)}) collective-permute-start(f32[8,2,1,64]{2,0,3,1:T(8,128)S(1)} %get-tuple-element.36), channel_id=1, source_target_pairs={{0,16},{16,0},{1,17},{17,1},{2,18},{18,2},{3,19},{19,3},{4,20},{20... | collective-permute-start | bytes 12296 | tf_op jit(solution)/shard_map/ppermute | solution.py:20
  241.2 3.6 collective-permute-start.26
  243.2 6.5 %collective-permute-start.27 = (f32[8,2,514,1]{2,0,3,1:T(8,128)S(1)}, f32[8,2,514,1]{2,0,3,1:T(8,128)S(1)}, u32[]{:S(2)}, u32[]{:S(2)}) collective-permute-start(f32[8,2,514,1]{2,0,3,1:T(8,128)S(1)} %get-tuple-element.18), channel_id=1, source_target_pairs={{0,1},{1,2},{2,3},{3,4},{4,5},{5,6},{6,7},{7,8},{8,9},{9,10},{10,1... | collective-permute-start | bytes 98696 | tf_op jit(solution)/shard_map/ppermute | solution.py:20
  255.3 23.6 %copy-start.5 = (f32[8,2,512,64]{2,0,3,1:T(8,128)}, f32[8,2,512,64]{2,0,3,1:T(8,128)S(1)}, u32[]{:S(2)}) copy-start(f32[8,2,512,64]{2,0,3,1:T(8,128)S(1)} %get-tuple-element.76) | copy-start | bytes 6291460
  256.6 14.8 %collective-permute-start.28 = (f32[8,2,1,64]{2,0,3,1:T(8,128)}, f32[8,2,1,64]{2,0,3,1:T(8,128)S(1)}, u32[]{:S(2)}, u32[]{:S(2)}) collective-permute-start(f32[8,2,1,64]{2,0,3,1:T(8,128)} %get-tuple-element.33), channel_id=1, source_target_pairs={{16,0},{0,16},{17,1},{1,17},{18,2},{2,18},{19,3},{3,19},{20,4},{4,... | collective-permute-start | bytes 12296 | tf_op jit(solution)/shard_map/ppermute | solution.py:22
  258.2 18.9 %collective-permute-start.29 = (f32[8,2,1,64]{2,0,3,1:T(8,128)}, f32[8,2,1,64]{2,0,3,1:T(8,128)S(1)}, u32[]{:S(2)}, u32[]{:S(2)}) collective-permute-start(f32[8,2,1,64]{2,0,3,1:T(8,128)} %get-tuple-element.32), channel_id=1, source_target_pairs={{0,16},{16,0},{1,17},{17,1},{2,18},{18,2},{3,19},{19,3},{4,20},{20... | collective-permute-start | bytes 12296 | tf_op jit(solution)/shard_map/ppermute | solution.py:20
  277.0 8.0 %copy-start.12 = (f32[8,2,512,64]{2,0,3,1:T(8,128)S(1)}, f32[8,2,512,64]{2,0,3,1:T(8,128)}, u32[]{:S(2)}) copy-start(f32[8,2,512,64]{2,0,3,1:T(8,128)} %get-tuple-element.75) | copy-start | bytes 6291460
  277.1 3.4 collective-permute-start.30
  278.9 6.1 %copy-start.4 = (f32[8,2,512,64]{2,0,3,1:T(8,128)S(1)}, f32[8,2,512,64]{2,0,3,1:T(8,128)}, u32[]{:S(2)}) copy-start(f32[8,2,512,64]{2,0,3,1:T(8,128)} %copy-done.3) | copy-start | bytes 6291460
  278.9 6.1 %copy-start.11 = (f32[8,2,512,64]{2,0,3,1:T(8,128)S(1)}, f32[8,2,512,64]{2,0,3,1:T(8,128)}, u32[]{:S(2)}) copy-start(f32[8,2,512,64]{2,0,3,1:T(8,128)} %get-tuple-element.73) | copy-start | bytes 6291460
  278.9 6.1 %collective-permute-start.31 = (f32[8,2,514,1]{2,0,3,1:T(8,128)S(1)}, f32[8,2,514,1]{2,0,3,1:T(8,128)S(1)}, u32[]{:S(2)}, u32[]{:S(2)}) collective-permute-start(f32[8,2,514,1]{2,0,3,1:T(8,128)S(1)} %get-tuple-element.16), channel_id=1, source_target_pairs={{0,1},{1,2},{2,3},{3,4},{4,5},{5,6},{6,7},{7,8},{8,9},{9,10},{10,1... | collective-permute-start | bytes 98696 | tf_op jit(solution)/shard_map/ppermute | solution.py:20
  293.8 3.8 copy-start.1
  299.5 71.0 %copy-start.2 = (f32[8,2,512,64]{2,0,3,1:T(8,128)S(1)}, f32[8,2,512,64]{2,0,3,1:T(8,128)}, u32[]{:S(2)}) copy-start(f32[8,2,512,64]{2,0,3,1:T(8,128)} %copy-done.1) | copy-start | bytes 6291460
  299.5 71.0 %all-gather.3.cloned.1.call-start = ((), (), s32[]{:S(2)}) async-start(), calls=%async_computation.3 | async-start | bytes 6291456 | tf_op jit(solution)/shard_map/all_gather | solution.py:64
  300.2 146.8 %all-gather.5.cloned.1.call-start = ((), (), s32[]{:S(2)}) async-start(), calls=%async_computation.5 | async-start | bytes 8912896 | tf_op jit(solution)/shard_map/all_gather | solution.py:77
  314.2 196.8 %reduce-scatter.6.cloned.1.call-start = ((), (), s32[]{:S(2)}) async-start(), calls=%async_computation.4 | async-start | bytes 2228224 | tf_op jit(solution)/shard_map/reduce_scatter | solution.py:70
  380.2 143.6 %reduce-scatter.8.cloned.1.call-start = ((), (), s32[]{:S(2)}) async-start(), calls=%async_computation.6 | async-start | bytes 393216 | tf_op jit(solution)/shard_map/reduce_scatter | solution.py:80
  453.9 58.7 %copy-start.7 = (bf16[1024,128]{1,0:T(8,128)(2,1)S(1)}, bf16[1024,128]{1,0:T(8,128)(2,1)}, u32[]{:S(2)}) copy-start(bf16[1024,128]{1,0:T(8,128)(2,1)} %param.11) | copy-start | bytes 786436
Sparse Core Ops, SparseCore 0:
  299.6 11.9 reduce-scatter.9
  313.8 56.7 all-gather.2
  372.7 74.2 all-gather.4
  450.6 60.3 reduce-scatter.5
  513.1 10.6 reduce-scatter.7
where the time goes:
time: 539 us; the launch traced here: 532 us
  waiting for transfers between devices  387 us (72%)
  matrix products  68 us (13%)
  starting transfers between devices  36.2 us (7%)
  local copies, waits for them, and re-layouts  23 us (4%)
  between operations  14.3 us (3%)
    ppermute x16, waiting for transfers between devices, with_halo(): lax.ppermute(head, axis, [((i + 1) % count, i) for i in range(count)])  111 us
    ppermute x16, waiting for transfers between devices, with_halo(): lax.ppermute(tail, axis, [(i, (i + 1) % count) for i in range(count)])  86 us
    all_gather x1, waiting for transfers between devices, shards(): incoming = lax.all_gather(projected, ('grp', 'gz'), axis=3, tiled=True)  64.2 us
    all_gather x1, waiting for transfers between devices, shards(): lax.all_gather(state, 'sim', axis=2, tiled=True)  56.1 us
    reduce_scatter x1, waiting for transfers between devices, shards(): lax.psum_scatter(gram_rows, ('grp', 'gz'), scatter_dimension=1, tiled=True)  51.4 us
    dot_general x8, matrix products, rates(): jnp.einsum('fg,gzxy->fzxy', coupling, jnp.tanh(center), precision=highest)  45.2 us
    ppermute x16, starting transfers between devices, with_halo(): lax.ppermute(head, axis, [((i + 1) % count, i) for i in range(count)])  31.4 us
    unnamed x6, waiting for transfers between devices  12.1 us
  transfers between devices with their start and end apart: 37, of which 37 were waited for; matrix products, arithmetic and copies ran while one was open for 7% of the time, Pallas kernels for 0%

commit v1 on v0

--- a/solution.py
+++ b/solution.py
@@ -8,6 +8,24 @@
 STEPS = 2
 time_step = 1.0
 highest = lax.Precision.HIGHEST
+
+
+def on_each_block(value, axis, dim, apply, out_dim):
+    count, index, span = (lax.axis_size(axis), lax.axis_index(axis), value.shape[dim])
+    upward = [(i, (i + 1) % count) for i in range(count)]
+    current, out = (value, None)
+    for step in range(count):
+        owner = (index - step) % count
+        coming = lax.ppermute(current, axis, upward) if step < count - 1 else None
+        made = apply(current, owner * span)
+        length = made.shape[out_dim]
+        if out is None:
+            out = jnp.zeros(
+                (*made.shape[:out_dim], count * length, *made.shape[out_dim + 1 :]), made.dtype
+            )
+        out = lax.dynamic_update_slice_in_dim(out, made, owner * length, axis=out_dim)
+        current = coming
+    return out
 
 
 def with_halo(cells, sides, width):
@@ -60,8 +78,12 @@
     x_rows = state.shape[2]
     basis_xf = basis_x.astype(jnp.float32)
     basis_yf = basis_y.astype(jnp.float32)
-    block = jnp.einsum(
-        "fzxy,fzwy->xw", state, lax.all_gather(state, "sim", axis=2, tiled=True), precision=highest
+    block = on_each_block(
+        state,
+        "sim",
+        2,
+        lambda part, offset: jnp.einsum("fzxy,fzwy->xw", state, part, precision=highest),
+        1,
     )
     gram_rows = block
     own_basis = lax.dynamic_slice_in_dim(basis_xf, lax.axis_index("sim") * x_rows, x_rows, 0)

time: 539 us -> 480 us (0.89)
  waiting for transfers between devices: 387 us -> 326 us
    all_gather x1 -> x0, waiting for transfers between devices: 56.1 us -> none  [shards(): lax.all_gather(state, 'sim', axis=2, tiled=True)]
    all_gather x1, waiting for transfers between devices: 64.2 us -> 17.9 us  [shards(): incoming = lax.all_gather(projected, ('grp', 'gz'), axis=3, tiled=True)]
    ppermute x0 -> x1, waiting for transfers between devices: none -> 40.9 us  [on_each_block(): coming = lax.ppermute(current, axis, upward) if step < count - 1 else None]
    unnamed x6 -> x5, waiting for transfers between devices: 12.1 us -> 12.2 us
  transfers between devices with their start and end apart: 37 -> 37, of which waited for: 37 -> 37; matrix products, arithmetic and copies ran while one was open for 7% -> 8% of each run, Pallas kernels for 0% -> 0%
where the time goes in v1:
time: 480 us; the launch traced here: 474 us
  waiting for transfers between devices  326 us (68%)
  matrix products  69 us (14%)
  starting transfers between devices  36.7 us (8%)
  local copies, waits for them, and re-layouts  24.4 us (5%)
  between operations  14.3 us (3%)
    ppermute x16, waiting for transfers between devices, with_halo(): lax.ppermute(head, axis, [((i + 1) % count, i) for i in range(count)])  111 us
    ppermute x16, waiting for transfers between devices, with_halo(): lax.ppermute(tail, axis, [(i, (i + 1) % count) for i in range(count)])  86 us
    reduce_scatter x1, waiting for transfers between devices, shards(): lax.psum_scatter(gram_rows, ('grp', 'gz'), scatter_dimension=1, tiled=True)  51.5 us
    dot_general x8, matrix products, rates(): jnp.einsum('fg,gzxy->fzxy', coupling, jnp.tanh(center), precision=highest)  45.2 us
    ppermute x1, waiting for transfers between devices, on_each_block(): coming = lax.ppermute(current, axis, upward) if step < count - 1 else None  40.9 us
    ppermute x16, starting transfers between devices, with_halo(): lax.ppermute(head, axis, [((i + 1) % count, i) for i in range(count)])  31.4 us
    all_gather x1, waiting for transfers between devices, shards(): incoming = lax.all_gather(projected, ('grp', 'gz'), axis=3, tiled=True)  17.9 us
    unnamed x5, waiting for transfers between devices  12.2 us
  transfers between devices with their start and end apart: 37, of which 37 were waited for; matrix products, arithmetic and copies ran while one was open for 8% of the time, Pallas kernels for 0%

profile of v1, /device:TPU:0, one launch (start us, length us, event | category | flops | bytes accessed | tf_op | source)
XLA Modules:
  0.0 473.9 jit_solution(1204799050187514679)
XLA Ops:
  7.2 2.8 copy.69
  10.3 3.1 collective-permute-start
  13.6 12.5 %collective-permute-done = f32[8,2,1,64]{2,0,3,1:T(8,128)S(1)} collective-permute-done((f32[8,2,1,64]{2,0,3,1:T(8,128)S(1)}, f32[8,2,1,64]{2,0,3,1:T(8,128)S(1)}, u32[]{:S(2)}, u32[]{:S(2)}) %collective-permute-start) | collective-permute-done | bytes 4128 | tf_op jit(solution)/shard_map/ppermute | solution.py:40
  26.1 10.4 %collective-permute-done.1 = f32[8,2,1,64]{2,0,3,1:T(8,128)S(1)} collective-permute-done((f32[8,2,1,64]{2,0,3,1:T(8,128)S(1)}, f32[8,2,1,64]{2,0,3,1:T(8,128)S(1)}, u32[]{:S(2)}, u32[]{:S(2)}) %collective-permute-start.1) | collective-permute-done | bytes 4128 | tf_op jit(solution)/shard_map/ppermute | solution.py:38
  36.6 3.4 collective-permute-start.2
  41.6 4.4 collective-permute-done.3
  46.1 5.2 %multiply_add_fusion.3 = (f32[8,2,512,64]{2,0,3,1:T(8,128)S(1)}, f32[8,2,512,64]{2,0,3,1:T(8,128)S(1)}) fusion(f32[8,2,512,64]{2,3,1,0:T(8,128)S(1)} %copy-done.4, f32[8,2,512,64]{2,3,1,0:T(8,128)S(1)} %tanh.24, f32[8,8]{1,0:T(8,128)S(1)} %copy-done.7, f32[8]{0:T(128)S(1)} %get-tuple-element.65, f32[8]{0:T(128)S(1)} %get-tuple-element.64, ...), kind=kOutput, calls=%fused_computation.163 | convolution fusion | flops 63963136 | bytes 12657248 | tf_op jit(solution)/shard_map/fg,gzxy->fzxy/dot_general | solution.py:59
  51.5 1.6 collective-permute-start.4
  53.6 12.5 %collective-permute-done.4 = f32[8,2,1,64]{2,0,3,1:T(8,128)S(1)} collective-permute-done((f32[8,2,1,64]{2,0,3,1:T(8,128)S(1)}, f32[8,2,1,64]{2,0,3,1:T(8,128)S(1)}, u32[]{:S(2)}, u32[]{:S(2)}) %collective-permute-start.4) | collective-permute-done | bytes 4128 | tf_op jit(solution)/shard_map/ppermute | solution.py:40
  66.1 5.6 %collective-permute-done.5 = f32[8,2,1,64]{2,0,3,1:T(8,128)S(1)} collective-permute-done((f32[8,2,1,64]{2,0,3,1:T(8,128)S(1)}, f32[8,2,1,64]{2,0,3,1:T(8,128)S(1)}, u32[]{:S(2)}, u32[]{:S(2)}) %collective-permute-start.5) | collective-permute-done | bytes 4128 | tf_op jit(solution)/shard_map/ppermute | solution.py:38
  71.9 4.1 collective-permute-start.6
  77.7 4.6 collective-permute-done.7
  82.3 4.5 multiply_add_fusion.2
  87.0 1.6 collective-permute-start.8
  89.1 12.5 %collective-permute-done.8 = f32[8,2,1,64]{2,0,3,1:T(8,128)S(1)} collective-permute-done((f32[8,2,1,64]{2,0,3,1:T(8,128)S(1)}, f32[8,2,1,64]{2,0,3,1:T(8,128)S(1)}, u32[]{:S(2)}, u32[]{:S(2)}) %collective-permute-start.8) | collective-permute-done | bytes 4128 | tf_op jit(solution)/shard_map/ppermute | solution.py:40
  101.6 5.6 %collective-permute-done.9 = f32[8,2,1,64]{2,0,3,1:T(8,128)S(1)} collective-permute-done((f32[8,2,1,64]{2,0,3,1:T(8,128)S(1)}, f32[8,2,1,64]{2,0,3,1:T(8,128)S(1)}, u32[]{:S(2)}, u32[]{:S(2)}) %collective-permute-start.9) | collective-permute-done | bytes 4128 | tf_op jit(solution)/shard_map/ppermute | solution.py:38
  107.3 2.7 collective-permute-start.10
  111.7 4.4 collective-permute-done.11
  116.1 4.9 %copy_add_fusion = (f32[8,2,512,64]{2,0,3,1:T(8,128)S(1)}, f32[8,2,512,64]{2,0,3,1:T(8,128)S(1)}) fusion(f32[8,2,512,64]{2,3,1,0:T(8,128)S(1)} %copy-done.4, f32[8,8]{1,0:T(8,128)S(1)} %copy-done.7, f32[8,2,512,64]{2,0,3,1:T(8,128)S(1)} %get-tuple-element.68, f32[8]{0:T(128)S(1)} %get-tuple-element.65, f32[8]{0:T(128)S(1)} %get-tuple-element.64, ...), kind=kOutput, calls=%fused_computation.217 | convolution fusion | flops 63438848 | bytes 10560096 | tf_op jit(solution)/shard_map/fg,gzxy->fzxy/dot_general | solution.py:59
  121.2 1.6 collective-permute-start.12
  123.3 12.5 %collective-permute-done.12 = f32[8,2,1,64]{2,0,3,1:T(8,128)S(1)} collective-permute-done((f32[8,2,1,64]{2,0,3,1:T(8,128)S(1)}, f32[8,2,1,64]{2,0,3,1:T(8,128)S(1)}, u32[]{:S(2)}, u32[]{:S(2)}) %collective-permute-start.12) | collective-permute-done | bytes 4128 | tf_op jit(solution)/shard_map/ppermute | solution.py:40
  135.8 5.6 %collective-permute-done.13 = f32[8,2,1,64]{2,0,3,1:T(8,128)S(1)} collective-permute-done((f32[8,2,1,64]{2,0,3,1:T(8,128)S(1)}, f32[8,2,1,64]{2,0,3,1:T(8,128)S(1)}, u32[]{:S(2)}, u32[]{:S(2)}) %collective-permute-start.13) | collective-permute-done | bytes 4128 | tf_op jit(solution)/shard_map/ppermute | solution.py:38
  144.5 4.6 collective-permute-done.15
  149.2 5.1 %fusion.34 = f32[8,2,512,64]{2,0,3,1:T(8,128)S(1)} fusion(f32[8,1,512,64]{2,0,3,1:T(8,128)S(1)} %get-tuple-element.51, f32[8,1,512,64]{2,0,3,1:T(8,128)S(1)} %get-tuple-element.50, f32[8,2,514,1]{2,0,3,1:T(8,128)S(1)} %collective-permute-done.14, f32[8,2,1,64]{2,0,3,1:T(8,128)S(1)} %collective-permute-done.12, f32[8,2,512,64]{2,0,3,1:T(8,128)S(1)} %get-tuple-element.70, ...), kind=kOutput, calls=%fused_computation.42 | convolution fusion | flops 66584576 | bytes 14754400 | tf_op jit(solution)/shard_map/fg,gzxy->fzxy/dot_general | solution.py:59
  154.5 1.6 collective-permute-start.16
  156.6 12.5 %collective-permute-done.16 = f32[8,2,1,64]{2,0,3,1:T(8,128)S(1)} collective-permute-done((f32[8,2,1,64]{2,0,3,1:T(8,128)S(1)}, f32[8,2,1,64]{2,0,3,1:T(8,128)S(1)}, u32[]{:S(2)}, u32[]{:S(2)}) %collective-permute-start.16) | collective-permute-done | bytes 4128 | tf_op jit(solution)/shard_map/ppermute | solution.py:40
  169.1 5.6 %collective-permute-done.17 = f32[8,2,1,64]{2,0,3,1:T(8,128)S(1)} collective-permute-done((f32[8,2,1,64]{2,0,3,1:T(8,128)S(1)}, f32[8,2,1,64]{2,0,3,1:T(8,128)S(1)}, u32[]{:S(2)}, u32[]{:S(2)}) %collective-permute-start.17) | collective-permute-done | bytes 4128 | tf_op jit(solution)/shard_map/ppermute | solution.py:38
  176.0 1.5 collective-permute-done.18
  177.5 4.4 collective-permute-done.19
  181.9 5.4 %multiply_add_fusion.1 = (f32[8,2,512,64]{2,0,3,1:T(8,128)S(1)}, f32[8,2,512,64]{2,0,3,1:T(8,128)}) fusion(f32[8,2,512,64]{2,0,3,1:T(8,128)S(1)} %fusion.34, f32[8,8]{1,0:T(8,128)S(1)} %copy-done.7, f32[8]{0:T(128)S(1)} %get-tuple-element.65, f32[8]{0:T(128)S(1)} %get-tuple-element.64, f32[8,2,1,64]{2,0,3,1:T(8,128)S(1)} %collective-permute-done.16, ...), kind=kOutput, calls=%fused_computation.153 | convolution fusion | flops 63963136 | bytes 8462944 | tf_op jit(solution)/shard_map/fg,gzxy->fzxy/dot_general | solution.py:59
  187.5 1.6 collective-permute-start.20
  189.6 12.5 %collective-permute-done.20 = f32[8,2,1,64]{2,0,3,1:T(8,128)S(1)} collective-permute-done((f32[8,2,1,64]{2,0,3,1:T(8,128)S(1)}, f32[8,2,1,64]{2,0,3,1:T(8,128)S(1)}, u32[]{:S(2)}, u32[]{:S(2)}) %collective-permute-start.20) | collective-permute-done | bytes 4128 | tf_op jit(solution)/shard_map/ppermute | solution.py:40
  202.1 5.6 %collective-permute-done.21 = f32[8,2,1,64]{2,0,3,1:T(8,128)S(1)} collective-permute-done((f32[8,2,1,64]{2,0,3,1:T(8,128)S(1)}, f32[8,2,1,64]{2,0,3,1:T(8,128)S(1)}, u32[]{:S(2)}, u32[]{:S(2)}) %collective-permute-start.21) | collective-permute-done | bytes 4128 | tf_op jit(solution)/shard_map/ppermute | solution.py:38
  210.7 4.4 collective-permute-done.23
  215.1 5.6 %multiply_add_fusion = (f32[8,2,512,64]{2,0,3,1:T(8,128)S(1)}, f32[8,2,512,64]{2,0,3,1:T(8,128)}) fusion(f32[8,2,512,64]{2,0,3,1:T(8,128)S(1)} %fusion.34, f32[8,8]{1,0:T(8,128)S(1)} %copy-done.7, f32[8,2,512,64]{2,0,3,1:T(8,128)S(1)} %get-tuple-element.72, f32[8]{0:T(128)S(1)} %get-tuple-element.65, f32[8]{0:T(128)S(1)} %get-tuple-element.64, ...), kind=kOutput, calls=%fused_computation.150 | convolution fusion | flops 63963136 | bytes 10560096 | tf_op jit(solution)/shard_map/fg,gzxy->fzxy/dot_general | solution.py:59
  220.9 1.6 collective-permute-start.24
  223.0 12.5 %collective-permute-done.24 = f32[8,2,1,64]{2,0,3,1:T(8,128)S(1)} collective-permute-done((f32[8,2,1,64]{2,0,3,1:T(8,128)S(1)}, f32[8,2,1,64]{2,0,3,1:T(8,128)S(1)}, u32[]{:S(2)}, u32[]{:S(2)}) %collective-permute-start.24) | collective-permute-done | bytes 4128 | tf_op jit(solution)/shard_map/ppermute | solution.py:40
  235.5 5.6 %collective-permute-done.25 = f32[8,2,1,64]{2,0,3,1:T(8,128)S(1)} collective-permute-done((f32[8,2,1,64]{2,0,3,1:T(8,128)S(1)}, f32[8,2,1,64]{2,0,3,1:T(8,128)S(1)}, u32[]{:S(2)}, u32[]{:S(2)}) %collective-permute-start.25) | collective-permute-done | bytes 4128 | tf_op jit(solution)/shard_map/ppermute | solution.py:38
  241.2 1.9 collective-permute-start.26
  244.8 4.8 %collective-permute-done.27 = f32[8,2,514,1]{2,0,3,1:T(8,128)S(1)} collective-permute-done((f32[8,2,514,1]{2,0,3,1:T(8,128)S(1)}, f32[8,2,514,1]{2,0,3,1:T(8,128)S(1)}, u32[]{:S(2)}, u32[]{:S(2)}) %collective-permute-start.27) | collective-permute-done | bytes 32928 | tf_op jit(solution)/shard_map/ppermute | solution.py:38
  249.7 5.6 %fusion.171 = (f32[8,2,512,64]{2,0,3,1:T(8,128)S(1)}, f32[8,2,512,64]{2,0,3,1:T(8,128)}) fusion(f32[8,2,512,64]{2,0,3,1:T(8,128)S(1)} %fusion.34, f32[8,8]{1,0:T(8,128)S(1)} %copy-done.7, f32[8,2,512,64]{2,0,3,1:T(8,128)S(1)} %get-tuple-element.74, f32[8]{0:T(128)S(1)} %get-tuple-element.65, f32[8]{0:T(128)S(1)} %get-tuple-element.64, ...), kind=kOutput, calls=%fused_computation.234 | convolution fusion | flops 63438848 | bytes 10560096 | tf_op jit(solution)/shard_map/fg,gzxy->fzxy/dot_general | solution.py:59
  256.6 1.5 collective-permute-start.28
  258.6 12.7 %collective-permute-done.28 = f32[8,2,1,64]{2,0,3,1:T(8,128)S(1)} collective-permute-done((f32[8,2,1,64]{2,0,3,1:T(8,128)}, f32[8,2,1,64]{2,0,3,1:T(8,128)S(1)}, u32[]{:S(2)}, u32[]{:S(2)}) %collective-permute-start.28) | collective-permute-done | bytes 4128 | tf_op jit(solution)/shard_map/ppermute | solution.py:40
  271.4 5.6 %collective-permute-done.29 = f32[8,2,1,64]{2,0,3,1:T(8,128)S(1)} collective-permute-done((f32[8,2,1,64]{2,0,3,1:T(8,128)}, f32[8,2,1,64]{2,0,3,1:T(8,128)S(1)}, u32[]{:S(2)}, u32[]{:S(2)}) %collective-permute-start.29) | collective-permute-done | bytes 4128 | tf_op jit(solution)/shard_map/ppermute | solution.py:38
  277.1 1.8 collective-permute-start.30
  280.5 4.5 collective-permute-done.31
  285.0 8.8 %fusion.69 = f32[8,2,512,64]{2,0,3,1:T(8,128)S(1)} fusion(f32[8,2,512,64]{2,0,3,1:T(8,128)S(1)} %copy-done.2, f32[8,1,512,64]{2,0,3,1:T(8,128)S(1)} %get-tuple-element.35, f32[8,1,512,64]{2,0,3,1:T(8,128)S(1)} %get-tuple-element.34, f32[8,2,514,1]{2,0,3,1:T(8,128)S(1)} %collective-permute-done.30, f32[8,2,1,64]{2,0,3,1:T(8,128)S(1)} %collective-permute-done.28, ...), kind=kOutput, calls=%fused_computation.77 | convolution fusion | flops 66584576 | bytes 14754400 | tf_op jit(solution)/shard_map/fg,gzxy->fzxy/dot_general | solution.py:59
  293.8 1.9 convolution_bitcast_fusion
  295.7 1.9 copy.90
  297.6 1.7 reshape.21
  299.4 12.1 %reduce-scatter.10.cloned.1.call-done = f32[64,1024]{1,0:T(8,128)} async-done(((f32[128,1024]{1,0:T(8,128)}), f32[64,1024]{1,0:T(8,128)}) %reduce-scatter.10.cloned.1.call-update) | async-done | bytes 262160
  314.7 1.6 broadcast_in_dim.2
  316.3 4.5 fusion.94
  320.8 40.9 %collective-permute-done.32 = f32[8,2,512,64]{2,0,3,1:T(8,128)} collective-permute-done((f32[8,2,512,64]{2,0,3,1:T(8,128)S(1)}, f32[8,2,512,64]{2,0,3,1:T(8,128)}, u32[]{:S(2)}, u32[]{:S(2)}) %collective-permute-start.32) | collective-permute-done | bytes 2097184 | tf_op jit(solution)/shard_map/ppermute | solution.py:19
  361.7 6.2 %fusion.102 = f32[512,1024]{0,1:T(8,128)} fusion(f32[512,1024]{0,1:T(8,128)} %fusion.94, s32[]{:T(128)S(6)} %select_n.26, f32[8,2,512,64]{2,0,3,1:T(8,128)} %collective-permute-done.32, f32[8,2,512,64]{2,0,3,1:T(8,128)S(1)} %fusion.69), kind=kOutput, calls=%fused_computation.170 | convolution fusion | flops 3221225472 | bytes 5242884 | tf_op jit(solution)/shard_map/fzxy,fzwy->xw/dot_general | solution.py:85
  368.2 2.5 copy.81
  370.7 17.9 %all-gather.2.cloned.1.call-done = f32[8,2,64,1024]{2,0,1,3:T(8,128)} async-done(((f32[8,2,64,64]{2,0,1,3:T(8,128)}), f32[8,2,64,1024]{2,0,1,3:T(8,128)}) %all-gather.2.cloned.1.call-update) | async-done | bytes 4194320 | tf_op jit(solution)/shard_map/all_gather | solution.py:99
  388.6 6.9 %copy.78 = f32[8,2,64,1024]{3,2,1,0:T(8,128)} copy(f32[8,2,64,1024]{2,0,1,3:T(8,128)} %all-gather.2.cloned.1.call-done) | data formatting | bytes 8388608 | tf_op jit(solution)/shard_map/all_gather | solution.py:99
  395.4 5.8 %convolution_bitcast_fusion.1 = f32[64,1024]{1,0:T(8,128)} fusion(f32[8,2,64,1024]{3,2,1,0:T(8,128)} %copy.78, f32[8,2,64,64]{3,1,0,2:T(2,128)S(1)} %bitcast.97), kind=kOutput, calls=%fused_computation.172 | convolution fusion | flops 805306368 | bytes 4718592 | tf_op jit(solution)/shard_map/fzry,fzrv->yv/dot_general | solution.py:100
  401.2 51.5 %reduce-scatter.6.cloned.1.call-done = f32[512,64]{0,1:T(8,128)} async-done(((f32[512,1024]{0,1:T(8,128)}), f32[512,64]{0,1:T(8,128)}) %reduce-scatter.6.cloned.1.call-update) | async-done | bytes 131088 | tf_op jit(solution)/shard_map/reduce_scatter | solution.py:92
  452.7 1.6 broadcast_multiply_fusion.1
  454.3 5.5 %fusion.108 = f32[8,2,64,8]{2,3,1,0:T(8,128)} fusion(f32[8,2,64,1024]{3,2,1,0:T(8,128)} %copy.78, bf16[1024,128]{1,0:T(8,128)(2,1)S(1)} %copy-done.5, s32[]{:T(128)S(6)} %select_n.28), kind=kOutput, calls=%fused_computation.174 | convolution fusion | flops 100663296 | bytes 4489220 | tf_op jit(solution)/shard_map/vs,fzrv->fzrs/dot_general | solution.py:101
  459.7 5.8 %reduce-scatter.8.cloned.1.call-done = f32[64,512]{1,0:T(8,128)} async-done(((f32[64,1024]{1,0:T(8,128)}), f32[64,512]{1,0:T(8,128)}) %reduce-scatter.8.cloned.1.call-update) | async-done | bytes 131088 | tf_op jit(solution)/shard_map/reduce_scatter | solution.py:102
  465.6 1.6 broadcast_multiply_fusion
  (85 shorter events, 26.1 us)
Async XLA Ops:
  7.2 286.7 %copy-start = (bf16[1024,128]{1,0:T(8,128)(2,1)S(1)}, bf16[1024,128]{1,0:T(8,128)(2,1)}, u32[]{:S(2)}) copy-start(bf16[1024,128]{1,0:T(8,128)(2,1)} %param.10) | copy-start | bytes 786436
  7.2 304.4 %reduce-scatter.10.cloned.1.call-start = ((), (), s32[]{:S(2)}) async-start(), calls=%async_computation.6 | async-start | bytes 786432
  10.3 15.8 %collective-permute-start = (f32[8,2,1,64]{2,0,3,1:T(8,128)S(1)}, f32[8,2,1,64]{2,0,3,1:T(8,128)S(1)}, u32[]{:S(2)}, u32[]{:S(2)}) collective-permute-start(f32[8,2,1,64]{2,0,3,1:T(8,128)S(1)} %get-tuple-element.61), channel_id=1, source_target_pairs={{16,0},{0,16},{17,1},{1,17},{18,2},{2,18},{19,3},{3,19},{20,4},{4,... | collective-permute-start | bytes 12296 | tf_op jit(solution)/shard_map/ppermute | solution.py:40
  13.3 23.2 %collective-permute-start.1 = (f32[8,2,1,64]{2,0,3,1:T(8,128)S(1)}, f32[8,2,1,64]{2,0,3,1:T(8,128)S(1)}, u32[]{:S(2)}, u32[]{:S(2)}) collective-permute-start(f32[8,2,1,64]{2,0,3,1:T(8,128)S(1)} %get-tuple-element.60), channel_id=1, source_target_pairs={{0,16},{16,0},{1,17},{17,1},{2,18},{18,2},{3,19},{19,3},{4,20},{20... | collective-permute-start | bytes 12296 | tf_op jit(solution)/shard_map/ppermute | solution.py:38
  13.6 26.4 %copy-start.6 = (f32[2,8]{1,0:T(2,128)S(1)}, f32[2,8]{1,0:T(2,128)}, u32[]{:S(2)}) copy-start(f32[2,8]{1,0:T(2,128)} %param.8) | copy-start | bytes 196
  13.6 26.4 %copy-start.4 = (f32[8,2,512,64]{2,3,1,0:T(8,128)S(1)}, f32[8,2,512,64]{2,3,1,0:T(8,128)}, u32[]{:S(2)}) copy-start(f32[8,2,512,64]{2,3,1,0:T(8,128)} %param.6) | copy-start | bytes 6291460
  36.6 5.1 %collective-permute-start.2 = (f32[8,2,514,1]{2,0,3,1:T(8,128)S(1)}, f32[8,2,514,1]{2,0,3,1:T(8,128)S(1)}, u32[]{:S(2)}, u32[]{:S(2)}) collective-permute-start(f32[8,2,514,1]{2,0,3,1:T(8,128)S(1)} %get-tuple-element.31), channel_id=1, source_target_pairs={{1,0},{2,1},{3,2},{4,3},{5,4},{6,5},{7,6},{8,7},{9,8},{10,9},{11,1... | collective-permute-start | bytes 98696 | tf_op jit(solution)/shard_map/ppermute | solution.py:40
  40.0 6.1 %collective-permute-start.3 = (f32[8,2,514,1]{2,0,3,1:T(8,128)S(1)}, f32[8,2,514,1]{2,0,3,1:T(8,128)S(1)}, u32[]{:S(2)}, u32[]{:S(2)}) collective-permute-start(f32[8,2,514,1]{2,0,3,1:T(8,128)S(1)} %get-tuple-element.30), channel_id=1, source_target_pairs={{0,1},{1,2},{2,3},{3,4},{4,5},{5,6},{6,7},{7,8},{8,9},{9,10},{10,1... | collective-permute-start | bytes 98696 | tf_op jit(solution)/shard_map/ppermute | solution.py:38
  40.0 6.1 %copy-start.7 = (f32[8,8]{1,0:T(8,128)S(1)}, f32[8,8]{1,0:T(8,128)}, u32[]{:S(2)}) copy-start(f32[8,8]{1,0:T(8,128)} %param.9) | copy-start | bytes 772
  40.0 6.1 %copy-start.8 = (f32[8]{0:T(128)S(1)}, f32[8]{0:T(128)}, u32[]{:S(2)}) copy-start(f32[8]{0:T(128)} %param.7) | copy-start | bytes 100
  51.5 14.6 %collective-permute-start.4 = (f32[8,2,1,64]{2,0,3,1:T(8,128)S(1)}, f32[8,2,1,64]{2,0,3,1:T(8,128)S(1)}, u32[]{:S(2)}, u32[]{:S(2)}) collective-permute-start(f32[8,2,1,64]{2,0,3,1:T(8,128)S(1)} %get-tuple-element.57), channel_id=1, source_target_pairs={{16,0},{0,16},{17,1},{1,17},{18,2},{2,18},{19,3},{3,19},{20,4},{4,... | collective-permute-start | bytes 12296 | tf_op jit(solution)/shard_map/ppermute | solution.py:40
  53.1 18.6 %collective-permute-start.5 = (f32[8,2,1,64]{2,0,3,1:T(8,128)S(1)}, f32[8,2,1,64]{2,0,3,1:T(8,128)S(1)}, u32[]{:S(2)}, u32[]{:S(2)}) collective-permute-start(f32[8,2,1,64]{2,0,3,1:T(8,128)S(1)} %get-tuple-element.56), channel_id=1, source_target_pairs={{0,16},{16,0},{1,17},{17,1},{2,18},{18,2},{3,19},{19,3},{4,20},{20... | collective-permute-start | bytes 12296 | tf_op jit(solution)/shard_map/ppermute | solution.py:38
  71.9 5.8 %collective-permute-start.6 = (f32[8,2,514,1]{2,0,3,1:T(8,128)S(1)}, f32[8,2,514,1]{2,0,3,1:T(8,128)S(1)}, u32[]{:S(2)}, u32[]{:S(2)}) collective-permute-start(f32[8,2,514,1]{2,0,3,1:T(8,128)S(1)} %get-tuple-element.29), channel_id=1, source_target_pairs={{1,0},{2,1},{3,2},{4,3},{5,4},{6,5},{7,6},{8,7},{9,8},{10,9},{11,1... | collective-permute-start | bytes 98696 | tf_op jit(solution)/shard_map/ppermute | solution.py:40
  76.0 6.3 %collective-permute-start.7 = (f32[8,2,514,1]{2,0,3,1:T(8,128)S(1)}, f32[8,2,514,1]{2,0,3,1:T(8,128)S(1)}, u32[]{:S(2)}, u32[]{:S(2)}) collective-permute-start(f32[8,2,514,1]{2,0,3,1:T(8,128)S(1)} %get-tuple-element.28), channel_id=1, source_target_pairs={{0,1},{1,2},{2,3},{3,4},{4,5},{5,6},{6,7},{7,8},{8,9},{9,10},{10,1... | collective-permute-start | bytes 98696 | tf_op jit(solution)/shard_map/ppermute | solution.py:38
  87.0 14.6 %collective-permute-start.8 = (f32[8,2,1,64]{2,0,3,1:T(8,128)S(1)}, f32[8,2,1,64]{2,0,3,1:T(8,128)S(1)}, u32[]{:S(2)}, u32[]{:S(2)}) collective-permute-start(f32[8,2,1,64]{2,0,3,1:T(8,128)S(1)} %get-tuple-element.53), channel_id=1, source_target_pairs={{16,0},{0,16},{17,1},{1,17},{18,2},{2,18},{19,3},{3,19},{20,4},{4,... | collective-permute-start | bytes 12296 | tf_op jit(solution)/shard_map/ppermute | solution.py:40
  88.6 18.6 %collective-permute-start.9 = (f32[8,2,1,64]{2,0,3,1:T(8,128)S(1)}, f32[8,2,1,64]{2,0,3,1:T(8,128)S(1)}, u32[]{:S(2)}, u32[]{:S(2)}) collective-permute-start(f32[8,2,1,64]{2,0,3,1:T(8,128)S(1)} %get-tuple-element.52), channel_id=1, source_target_pairs={{0,16},{16,0},{1,17},{17,1},{2,18},{18,2},{3,19},{19,3},{4,20},{20... | collective-permute-start | bytes 12296 | tf_op jit(solution)/shard_map/ppermute | solution.py:38
  107.3 4.3 collective-permute-start.10
  110.0 6.1 %collective-permute-start.11 = (f32[8,2,514,1]{2,0,3,1:T(8,128)S(1)}, f32[8,2,514,1]{2,0,3,1:T(8,128)S(1)}, u32[]{:S(2)}, u32[]{:S(2)}) collective-permute-start(f32[8,2,514,1]{2,0,3,1:T(8,128)S(1)} %get-tuple-element.26), channel_id=1, source_target_pairs={{0,1},{1,2},{2,3},{3,4},{4,5},{5,6},{6,7},{7,8},{8,9},{9,10},{10,1... | collective-permute-start | bytes 98696 | tf_op jit(solution)/shard_map/ppermute | solution.py:38
  121.2 14.6 %collective-permute-start.12 = (f32[8,2,1,64]{2,0,3,1:T(8,128)S(1)}, f32[8,2,1,64]{2,0,3,1:T(8,128)S(1)}, u32[]{:S(2)}, u32[]{:S(2)}) collective-permute-start(f32[8,2,1,64]{2,0,3,1:T(8,128)S(1)} %get-tuple-element.49), channel_id=1, source_target_pairs={{16,0},{0,16},{17,1},{1,17},{18,2},{2,18},{19,3},{3,19},{20,4},{4,... | collective-permute-start | bytes 12296 | tf_op jit(solution)/shard_map/ppermute | solution.py:40
  122.8 18.6 %collective-permute-start.13 = (f32[8,2,1,64]{2,0,3,1:T(8,128)S(1)}, f32[8,2,1,64]{2,0,3,1:T(8,128)S(1)}, u32[]{:S(2)}, u32[]{:S(2)}) collective-permute-start(f32[8,2,1,64]{2,0,3,1:T(8,128)S(1)} %get-tuple-element.48), channel_id=1, source_target_pairs={{0,16},{16,0},{1,17},{17,1},{2,18},{18,2},{3,19},{19,3},{4,20},{20... | collective-permute-start | bytes 12296 | tf_op jit(solution)/shard_map/ppermute | solution.py:38
  141.5 3.0 collective-permute-start.14
  142.9 6.3 %collective-permute-start.15 = (f32[8,2,514,1]{2,0,3,1:T(8,128)S(1)}, f32[8,2,514,1]{2,0,3,1:T(8,128)S(1)}, u32[]{:S(2)}, u32[]{:S(2)}) collective-permute-start(f32[8,2,514,1]{2,0,3,1:T(8,128)S(1)} %get-tuple-element.24), channel_id=1, source_target_pairs={{0,1},{1,2},{2,3},{3,4},{4,5},{5,6},{6,7},{7,8},{8,9},{9,10},{10,1... | collective-permute-start | bytes 98696 | tf_op jit(solution)/shard_map/ppermute | solution.py:38
  154.3 95.4 %copy-start.1 = (f32[8,2,512,64]{2,0,3,1:T(8,128)}, f32[8,2,512,64]{2,0,3,1:T(8,128)S(1)}, u32[]{:S(2)}) copy-start(f32[8,2,512,64]{2,0,3,1:T(8,128)S(1)} %fusion.34) | copy-start | bytes 6291460
  154.5 14.6 %collective-permute-start.16 = (f32[8,2,1,64]{2,0,3,1:T(8,128)S(1)}, f32[8,2,1,64]{2,0,3,1:T(8,128)S(1)}, u32[]{:S(2)}, u32[]{:S(2)}) collective-permute-start(f32[8,2,1,64]{2,0,3,1:T(8,128)S(1)} %get-tuple-element.45), channel_id=1, source_target_pairs={{16,0},{0,16},{17,1},{1,17},{18,2},{2,18},{19,3},{3,19},{20,4},{4,... | collective-permute-start | bytes 12296 | tf_op jit(solution)/shard_map/ppermute | solution.py:40
  156.1 18.6 %collective-permute-start.17 = (f32[8,2,1,64]{2,0,3,1:T(8,128)S(1)}, f32[8,2,1,64]{2,0,3,1:T(8,128)S(1)}, u32[]{:S(2)}, u32[]{:S(2)}) collective-permute-start(f32[8,2,1,64]{2,0,3,1:T(8,128)S(1)} %get-tuple-element.44), channel_id=1, source_target_pairs={{0,16},{16,0},{1,17},{17,1},{2,18},{18,2},{3,19},{19,3},{4,20},{20... | collective-permute-start | bytes 12296 | tf_op jit(solution)/shard_map/ppermute | solution.py:38
  174.8 2.6 collective-permute-start.18
  175.8 6.1 %collective-permute-start.19 = (f32[8,2,514,1]{2,0,3,1:T(8,128)S(1)}, f32[8,2,514,1]{2,0,3,1:T(8,128)S(1)}, u32[]{:S(2)}, u32[]{:S(2)}) collective-permute-start(f32[8,2,514,1]{2,0,3,1:T(8,128)S(1)} %get-tuple-element.22), channel_id=1, source_target_pairs={{0,1},{1,2},{2,3},{3,4},{4,5},{5,6},{6,7},{7,8},{8,9},{9,10},{10,1... | collective-permute-start | bytes 98696 | tf_op jit(solution)/shard_map/ppermute | solution.py:38
  187.5 14.6 %collective-permute-start.20 = (f32[8,2,1,64]{2,0,3,1:T(8,128)S(1)}, f32[8,2,1,64]{2,0,3,1:T(8,128)S(1)}, u32[]{:S(2)}, u32[]{:S(2)}) collective-permute-start(f32[8,2,1,64]{2,0,3,1:T(8,128)S(1)} %get-tuple-element.41), channel_id=1, source_target_pairs={{16,0},{0,16},{17,1},{1,17},{18,2},{2,18},{19,3},{3,19},{20,4},{4,... | collective-permute-start | bytes 12296 | tf_op jit(solution)/shard_map/ppermute | solution.py:40
  189.1 18.6 %collective-permute-start.21 = (f32[8,2,1,64]{2,0,3,1:T(8,128)S(1)}, f32[8,2,1,64]{2,0,3,1:T(8,128)S(1)}, u32[]{:S(2)}, u32[]{:S(2)}) collective-permute-start(f32[8,2,1,64]{2,0,3,1:T(8,128)S(1)} %get-tuple-element.40), channel_id=1, source_target_pairs={{0,16},{16,0},{1,17},{17,1},{2,18},{18,2},{3,19},{19,3},{4,20},{20... | collective-permute-start | bytes 12296 | tf_op jit(solution)/shard_map/ppermute | solution.py:38
  207.8 2.8 collective-permute-start.22
  209.0 6.1 %collective-permute-start.23 = (f32[8,2,514,1]{2,0,3,1:T(8,128)S(1)}, f32[8,2,514,1]{2,0,3,1:T(8,128)S(1)}, u32[]{:S(2)}, u32[]{:S(2)}) collective-permute-start(f32[8,2,514,1]{2,0,3,1:T(8,128)S(1)} %get-tuple-element.20), channel_id=1, source_target_pairs={{0,1},{1,2},{2,3},{3,4},{4,5},{5,6},{6,7},{7,8},{8,9},{9,10},{10,1... | collective-permute-start | bytes 98696 | tf_op jit(solution)/shard_map/ppermute | solution.py:38
  220.9 14.6 %collective-permute-start.24 = (f32[8,2,1,64]{2,0,3,1:T(8,128)S(1)}, f32[8,2,1,64]{2,0,3,1:T(8,128)S(1)}, u32[]{:S(2)}, u32[]{:S(2)}) collective-permute-start(f32[8,2,1,64]{2,0,3,1:T(8,128)S(1)} %get-tuple-element.37), channel_id=1, source_target_pairs={{16,0},{0,16},{17,1},{1,17},{18,2},{2,18},{19,3},{3,19},{20,4},{4,... | collective-permute-start | bytes 12296 | tf_op jit(solution)/shard_map/ppermute | solution.py:40
  222.5 18.6 %collective-permute-start.25 = (f32[8,2,1,64]{2,0,3,1:T(8,128)S(1)}, f32[8,2,1,64]{2,0,3,1:T(8,128)S(1)}, u32[]{:S(2)}, u32[]{:S(2)}) collective-permute-start(f32[8,2,1,64]{2,0,3,1:T(8,128)S(1)} %get-tuple-element.36), channel_id=1, source_target_pairs={{0,16},{16,0},{1,17},{17,1},{2,18},{18,2},{3,19},{19,3},{4,20},{20... | collective-permute-start | bytes 12296 | tf_op jit(solution)/shard_map/ppermute | solution.py:38
  241.2 3.6 collective-permute-start.26
  243.2 6.5 %collective-permute-start.27 = (f32[8,2,514,1]{2,0,3,1:T(8,128)S(1)}, f32[8,2,514,1]{2,0,3,1:T(8,128)S(1)}, u32[]{:S(2)}, u32[]{:S(2)}) collective-permute-start(f32[8,2,514,1]{2,0,3,1:T(8,128)S(1)} %get-tuple-element.18), channel_id=1, source_target_pairs={{0,1},{1,2},{2,3},{3,4},{4,5},{5,6},{6,7},{7,8},{8,9},{9,10},{10,1... | collective-permute-start | bytes 98696 | tf_op jit(solution)/shard_map/ppermute | solution.py:38
  255.3 23.6 %copy-start.3 = (f32[8,2,512,64]{2,0,3,1:T(8,128)}, f32[8,2,512,64]{2,0,3,1:T(8,128)S(1)}, u32[]{:S(2)}) copy-start(f32[8,2,512,64]{2,0,3,1:T(8,128)S(1)} %get-tuple-element.76) | copy-start | bytes 6291460
  256.6 14.8 %collective-permute-start.28 = (f32[8,2,1,64]{2,0,3,1:T(8,128)}, f32[8,2,1,64]{2,0,3,1:T(8,128)S(1)}, u32[]{:S(2)}, u32[]{:S(2)}) collective-permute-start(f32[8,2,1,64]{2,0,3,1:T(8,128)} %get-tuple-element.33), channel_id=1, source_target_pairs={{16,0},{0,16},{17,1},{1,17},{18,2},{2,18},{19,3},{3,19},{20,4},{4,... | collective-permute-start | bytes 12296 | tf_op jit(solution)/shard_map/ppermute | solution.py:40
  258.1 18.9 %collective-permute-start.29 = (f32[8,2,1,64]{2,0,3,1:T(8,128)}, f32[8,2,1,64]{2,0,3,1:T(8,128)S(1)}, u32[]{:S(2)}, u32[]{:S(2)}) collective-permute-start(f32[8,2,1,64]{2,0,3,1:T(8,128)} %get-tuple-element.32), channel_id=1, source_target_pairs={{0,16},{16,0},{1,17},{17,1},{2,18},{18,2},{3,19},{19,3},{4,20},{20... | collective-permute-start | bytes 12296 | tf_op jit(solution)/shard_map/ppermute | solution.py:38
  277.0 8.0 %copy-start.10 = (f32[8,2,512,64]{2,0,3,1:T(8,128)S(1)}, f32[8,2,512,64]{2,0,3,1:T(8,128)}, u32[]{:S(2)}) copy-start(f32[8,2,512,64]{2,0,3,1:T(8,128)} %get-tuple-element.75) | copy-start | bytes 6291460
  277.1 3.4 collective-permute-start.30
  278.8 6.1 %copy-start.2 = (f32[8,2,512,64]{2,0,3,1:T(8,128)S(1)}, f32[8,2,512,64]{2,0,3,1:T(8,128)}, u32[]{:S(2)}) copy-start(f32[8,2,512,64]{2,0,3,1:T(8,128)} %copy-done.1) | copy-start | bytes 6291460
  278.9 6.1 %copy-start.9 = (f32[8,2,512,64]{2,0,3,1:T(8,128)S(1)}, f32[8,2,512,64]{2,0,3,1:T(8,128)}, u32[]{:S(2)}) copy-start(f32[8,2,512,64]{2,0,3,1:T(8,128)} %get-tuple-element.73) | copy-start | bytes 6291460
  278.9 6.1 %collective-permute-start.31 = (f32[8,2,514,1]{2,0,3,1:T(8,128)S(1)}, f32[8,2,514,1]{2,0,3,1:T(8,128)S(1)}, u32[]{:S(2)}, u32[]{:S(2)}) collective-permute-start(f32[8,2,514,1]{2,0,3,1:T(8,128)S(1)} %get-tuple-element.16), channel_id=1, source_target_pairs={{0,1},{1,2},{2,3},{3,4},{4,5},{5,6},{6,7},{7,8},{8,9},{9,10},{10,1... | collective-permute-start | bytes 98696 | tf_op jit(solution)/shard_map/ppermute | solution.py:38
  299.4 89.2 %all-gather.2.cloned.1.call-start = ((), (), s32[]{:S(2)}) async-start(), calls=%async_computation.4 | async-start | bytes 8912896 | tf_op jit(solution)/shard_map/all_gather | solution.py:99
  314.1 138.6 %reduce-scatter.6.cloned.1.call-start = ((), (), s32[]{:S(2)}) async-start(), calls=%async_computation.3 | async-start | bytes 2228224 | tf_op jit(solution)/shard_map/reduce_scatter | solution.py:92
  314.3 47.4 %collective-permute-start.32 = (f32[8,2,512,64]{2,0,3,1:T(8,128)S(1)}, f32[8,2,512,64]{2,0,3,1:T(8,128)}, u32[]{:S(2)}, u32[]{:S(2)}) collective-permute-start(f32[8,2,512,64]{2,0,3,1:T(8,128)S(1)} %fusion.69), channel_id=1, source_target_pairs={{0,16},{16,0},{1,17},{17,1},{2,18},{18,2},{3,19},{19,3},{4,20},{20... | collective-permute-start | bytes 6291464 | tf_op jit(solution)/shard_map/ppermute | solution.py:19
  367.9 97.7 %reduce-scatter.8.cloned.1.call-start = ((), (), s32[]{:S(2)}) async-start(), calls=%async_computation.5 | async-start | bytes 393216 | tf_op jit(solution)/shard_map/reduce_scatter | solution.py:102
  395.4 58.9 %copy-start.5 = (bf16[1024,128]{1,0:T(8,128)(2,1)S(1)}, bf16[1024,128]{1,0:T(8,128)(2,1)}, u32[]{:S(2)}) copy-start(bf16[1024,128]{1,0:T(8,128)(2,1)} %param.11) | copy-start | bytes 786436
Sparse Core Ops, SparseCore 0:
  299.5 11.9 reduce-scatter.9
  314.2 74.2 all-gather.1
  392.3 60.3 reduce-scatter.5
  454.8 10.7 reduce-scatter.7
